TPU v7x, 128 devices: a whole 4x4x4 slice. The times are simulated.
128 devices in a mesh: elec: 8 (over y_lo, z), cell: 16 (over y_hi, x, core).
Axes of the slice: x: 4, y: 4 (y_hi: 2, y_lo: 2; y = y_hi * 2 + y_lo), z: 4, core: 2. Of those that a mesh axis runs over, the one named last changes fastest.
Arguments:
- grads: bfloat16 [3, 1024, 2048], P(None, 'elec', 'cell'), may hold values from -6 to 6
- quads: int32 [32768, 4], P('elec'), may hold values from 0 to 1023, all different within a row
- volume: float32 [2048], P('cell'), may hold values from 0.5 to 2
- weight: float32 [32768], P('elec'), may hold values from 0.5 to 2
Outputs:
- hessian: float32 [2048, 2048], P('elec', 'cell')
Inputs may be any that keep to these rules, and one draw needn't show every extreme that they name: `quads`: each row names four different electrodes; every electrode appears in some row.
All inputs are finite; a program needn't handle non-finite values.
Results may differ from a plain program's by a relative error of at most 0.00096.
Values may be sent and summed in bfloat16 or wider, within the bound.
A program may use at most 64 MiB of HBM per device.

v0:
```python
import jax
import jax.numpy as jnp
from jax import lax
from jax.sharding import PartitionSpec as P


def inner_rows(left, right):
    return lax.dot_general(
        left, right, (((0,), (0,)), ((), ())), preferred_element_type=jnp.float32
    )


def per_device(grads, quads, volume, weight):
    measured_rows = quads.shape[0]
    piece = lax.all_gather(grads, "elec", axis=1, tiled=True)
    width = piece.shape[1]
    labels = lax.iota(jnp.int32, width)
    source_map = (
        (quads[:, 0:1] == labels).astype(jnp.float32)
        - (quads[:, 1:2] == labels).astype(jnp.float32)
    ).astype(jnp.bfloat16)
    receive_map = (
        (quads[:, 2:3] == labels).astype(jnp.float32)
        - (quads[:, 3:4] == labels).astype(jnp.float32)
    ).astype(jnp.bfloat16)
    source = jnp.einsum("me,kec->kmc", source_map, piece, preferred_element_type=jnp.float32)
    receiver = jnp.einsum("me,kec->kmc", receive_map, piece, preferred_element_type=jnp.float32)
    source, receiver = (source, receiver)
    dots = source[0] * receiver[0] + source[1] * receiver[1] + source[2] * receiver[2]
    scaled_rows = (weight[:, None] * -(volume[None, :] * dots)).astype(jnp.bfloat16)
    term = inner_rows(lax.all_gather(scaled_rows, "cell", axis=1, tiled=True), scaled_rows)
    summed_rows = lax.psum_scatter(term, "elec", scatter_dimension=0, tiled=True)
    return summed_rows / jnp.float32(measured_rows * lax.axis_size("elec"))


def solution(mesh):
    placed = (P(None, "elec", "cell"), P("elec", None), P("cell"), P("elec"))
    return jax.shard_map(
        per_device, mesh=mesh, in_specs=placed, out_specs=P("elec", "cell"), check_vma=False
    )
```

profile of v0, /device:TPU:0, one launch (start us, length us, event | category | flops | bytes accessed | tf_op | source)
XLA Modules:
  0.0 235.7 jit_solution(18083217160854926386)
XLA Ops:
  6.5 0.0 all-gather.2.cloned.1.call-start
  6.5 1.1 fusion.23
  7.6 31.4 %all_gather.6 = bf16[3,1024,128]{2,1,0:T(8,128)(2,1)S(1)} all-gather(bf16[3,128,128]{2,1,0:T(8,128)(2,1)} %param.4), channel_id=1, replica_groups=mesh['elec'=8,'cell'=16] {'elec'}, dimensions={1}, use_global_device_ids=true | all-gather | bytes 884736 | tf_op jit(solution)/shard_map/all_gather | solution.py:15
  39.0 6.9 %fusion.10 = f32[3,4096,128]{2,1,0:T(8,128)S(1)} fusion(bf16[3,1024,128]{2,1,0:T(8,128)(2,1)S(1)} %all_gather.6, s32[4096]{0:T(1024)S(1)} %bitcast.34, s32[4096]{0:T(1024)S(1)} %bitcast.35), kind=kOutput, calls=%fused_computation.14 | convolution fusion | flops 3246391296 | bytes 7110656 | tf_op jit(solution)/shard_map/me,kec->kmc/dot_general | solution.py:27
  45.9 0.0 copy-start
  45.9 0.0 copy-start.1
  45.9 6.9 %fusion.13 = f32[3,4096,128]{2,1,0:T(8,128)S(1)} fusion(bf16[3,1024,128]{2,1,0:T(8,128)(2,1)S(1)} %all_gather.6, s32[4096]{0:T(1024)S(1)} %bitcast.33, s32[4096]{0:T(1024)S(1)} %bitcast.32), kind=kOutput, calls=%fused_computation.15 | convolution fusion | flops 3246391296 | bytes 7110656 | tf_op jit(solution)/shard_map/me,kec->kmc/dot_general | solution.py:26
  52.8 0.0 copy-done
  52.9 0.0 copy-done.1
  52.9 1.5 fusion.21
  54.4 0.0 all-gather.2.cloned.1.call-update
  54.4 0.0 reduce-scatter.2.cloned.1.call-start
  54.5 123.3 %all-gather.2.cloned.1.call-done = bf16[4096,2048]{1,0:T(8,128)(2,1)} async-done(((bf16[4096,128]{1,0:T(8,128)(2,1)}), bf16[4096,2048]{1,0:T(8,128)(2,1)}) %all-gather.2.cloned.1.call-update) | async-done | bytes 16777232 | tf_op jit(solution)/shard_map/all_gather | solution.py:31
  177.8 11.6 %fusion.24 = f32[2048,128]{1,0:T(8,128)} fusion(bf16[4096,2048]{1,0:T(8,128)(2,1)} %all-gather.2.cloned.1.call-done, bf16[4096,128]{1,0:T(8,128)(2,1)} %fusion.21), kind=kOutput, calls=%fused_computation.28 | convolution fusion | flops 2147483648 | bytes 18874368 | tf_op jit(solution)/shard_map/dot_general | solution.py:8
  189.4 0.0 reduce-scatter.2.cloned.1.call-update
  189.4 37.9 %reduce-scatter.2.cloned.1.call-done = f32[256,128]{1,0:T(8,128)} async-done(((f32[2048,128]{1,0:T(8,128)}), f32[256,128]{1,0:T(8,128)}) %reduce-scatter.2.cloned.1.call-update) | async-done | bytes 131088 | tf_op jit(solution)/shard_map/reduce_scatter | solution.py:32
  227.3 1.6 broadcast_multiply_fusion
Async XLA Ops:
  6.5 171.2 %all-gather.2.cloned.1.call-start = ((), (), s32[]{:S(2)}) async-start(), calls=%async_computation.1 | async-start | bytes 17825792 | tf_op jit(solution)/shard_map/all_gather | solution.py:31
  45.9 7.0 %copy-start = (f32[4096]{0:T(1024)S(1)}, f32[4096]{0:T(1024)}, u32[]{:S(2)}) copy-start(f32[4096]{0:T(1024)} %param.7) | copy-start | bytes 49156
  45.9 7.0 %copy-start.1 = (f32[128]{0:T(128)S(1)}, f32[128]{0:T(128)}, u32[]{:S(2)}) copy-start(f32[128]{0:T(128)} %param.6) | copy-start | bytes 1540
  54.4 172.9 %reduce-scatter.2.cloned.1.call-start = ((), (), s32[]{:S(2)}) async-start(), calls=%async_computation.2 | async-start | bytes 1179648 | tf_op jit(solution)/shard_map/reduce_scatter | solution.py:32
Sparse Core Ops, SparseCore 0:
  54.5 123.1 all-gather.1
  189.5 37.7 reduce-scatter.1
where the time goes:
time: 236 us
  waiting for transfers between devices  161 us (68%)
  blocking collectives  31.4 us (13%)
  matrix products  25.4 us (11%)
  between operations  13.5 us (6%)
  other arithmetic  3.1 us (1%)
    all_gather x1, waiting for transfers between devices, per_device(): lax.all_gather(scaled_rows, 'cell', axis=1, tiled=True)  123 us
    reduce_scatter x1, waiting for transfers between devices, per_device(): lax.psum_scatter(term, 'elec', scatter_dimension=0, tiled=True)  37.9 us
    all_gather x1, blocking collectives, per_device(): piece = lax.all_gather(grads, 'elec', axis=1, tiled=True)  31.4 us
    dot_general x1, matrix products, inner_rows(): lax.dot_general(left, right, (((0,), (0,)), ((), ())), preferred_element_...  11.6 us
    dot_general x1, matrix products, per_device(): jnp.einsum('me,kec->kmc', source_map, piece, preferred_element_type=jnp.f...  6.94 us
    dot_general x1, matrix products, per_device(): jnp.einsum('me,kec->kmc', receive_map, piece, preferred_element_type=jnp....  6.91 us
  transfers between devices with their start and end apart: 2, of which 2 were waited for; matrix products, arithmetic and copies ran while one was open for 0% of the time, Pallas kernels for 0%

commit v1 on v0

--- a/solution.py
+++ b/solution.py
@@ -2,6 +2,13 @@
 import jax.numpy as jnp
 from jax import lax
 from jax.sharding import PartitionSpec as P
+
+
+def all_by_exchange(x, name, d):
+    size = lax.axis_size(name)
+    parts = jnp.stack([x for _ in range(size)])
+    parts = lax.all_to_all(parts, name, split_axis=0, concat_axis=0)
+    return jnp.concatenate(parts, axis=d)
 
 
 def inner_rows(left, right):
@@ -12,7 +19,7 @@
 
 def per_device(grads, quads, volume, weight):
     measured_rows = quads.shape[0]
-    piece = lax.all_gather(grads, "elec", axis=1, tiled=True)
+    piece = all_by_exchange(grads, "elec", 1)
     width = piece.shape[1]
     labels = lax.iota(jnp.int32, width)
     source_map = (

time: 236 us -> 223 us (0.945)
  blocking collectives: 31.4 us -> 0 us
  waiting for transfers between devices: 161 us -> 171 us
  starting transfers between devices: 0.04 us -> 6.52 us
    all_gather x1 -> x0, blocking collectives: 31.4 us -> none  [per_device(): piece = lax.all_gather(grads, 'elec', axis=1, tiled=True)]
    all_to_all x0 -> x1, waiting for transfers between devices: none -> 10.9 us  [all_by_exchange(): parts = lax.all_to_all(parts, name, split_axis=0, concat_axis=0)]
    all_to_all x0 -> x1, starting transfers between devices: none -> 6.44 us  [all_by_exchange(): parts = lax.all_to_all(parts, name, split_axis=0, concat_axis=0)]
  transfers between devices with their start and end apart: 2 -> 3, of which waited for: 2 -> 3; matrix products, arithmetic and copies ran while one was open for 0% -> 0% of each run, Pallas kernels for 0% -> 0%
where the time goes in v1:
time: 223 us
  waiting for transfers between devices  171 us (77%)
  matrix products  25.6 us (11%)
  between operations  13.5 us (6%)
  starting transfers between devices  6.52 us (3%)
  other arithmetic  3.09 us (1%)
  local copies, waits for them, and re-layouts  3.08 us (1%)
    all_gather x1, waiting for transfers between devices, per_device(): lax.all_gather(scaled_rows, 'cell', axis=1, tiled=True)  122 us
    reduce_scatter x1, waiting for transfers between devices, per_device(): lax.psum_scatter(term, 'elec', scatter_dimension=0, tiled=True)  37.9 us
    dot_general x1, matrix products, inner_rows(): lax.dot_general(left, right, (((0,), (0,)), ((), ())), preferred_element_...  11.6 us
    all_to_all x1, waiting for transfers between devices, all_by_exchange(): parts = lax.all_to_all(parts, name, split_axis=0, concat_axis=0)  10.9 us
    dot_general x1, matrix products, per_device(): jnp.einsum('me,kec->kmc', receive_map, piece, preferred_element_type=jnp....  7 us
    dot_general x1, matrix products, per_device(): jnp.einsum('me,kec->kmc', source_map, piece, preferred_element_type=jnp.f...  6.98 us
    all_to_all x1, starting transfers between devices, all_by_exchange(): parts = lax.all_to_all(parts, name, split_axis=0, concat_axis=0)  6.44 us
  transfers between devices with their start and end apart: 3, of which 3 were waited for; matrix products, arithmetic and copies ran while one was open for 0% of the time, Pallas kernels for 0%

profile of v1, /device:TPU:0, one launch (start us, length us, event | category | flops | bytes accessed | tf_op | source)
XLA Modules:
  0.0 222.6 jit_solution(7136416878336491439)
XLA Ops:
  6.5 2.0 stack.2
  8.5 6.4 %all-to-all-start = ((bf16[8,3,128,128]{3,2,1,0:T(8,128)(2,1)}), bf16[8,3,128,128]{3,2,1,0:T(8,128)(2,1)S(1)}, u32[]{:S(2)}, u32[]{:S(2)}) async-start(bf16[8,3,128,128]{3,2,1,0:T(8,128)(2,1)} %stack.2), calls=%async_computation | async-start | bytes 1572864 | tf_op jit(solution)/shard_map/all_to_all | solution.py:10
  14.9 0.0 all-gather.2.cloned.1.call-start
  15.0 1.1 fusion.23
  16.0 10.9 %all-to-all-done = bf16[8,3,128,128]{3,2,1,0:T(8,128)(2,1)S(1)} async-done(((bf16[8,3,128,128]{3,2,1,0:T(8,128)(2,1)}), bf16[8,3,128,128]{3,2,1,0:T(8,128)(2,1)S(1)}, u32[]{:S(2)}, u32[]{:S(2)}) %all-to-all-start) | async-done | bytes 786464 | tf_op jit(solution)/shard_map/all_to_all | solution.py:10
  26.9 0.1 copy.5
  27.0 7.0 %fusion.10 = f32[3,4096,128]{2,1,0:T(8,128)S(1)} fusion(bf16[3,1024,128]{2,1,0:T(8,128)(2,1)S(1)} %bitcast.35, s32[4096]{0:T(1024)S(1)} %bitcast.39, s32[4096]{0:T(1024)S(1)} %bitcast.40), kind=kOutput, calls=%fused_computation.14 | convolution fusion | flops 3246391296 | bytes 7110656 | tf_op jit(solution)/shard_map/me,kec->kmc/dot_general | solution.py:34
  34.0 0.0 copy-start
  34.0 0.0 copy-start.1
  34.0 7.0 %fusion.13 = f32[3,4096,128]{2,1,0:T(8,128)S(1)} fusion(bf16[3,1024,128]{2,1,0:T(8,128)(2,1)S(1)} %bitcast.36, s32[4096]{0:T(1024)S(1)} %bitcast.38, s32[4096]{0:T(1024)S(1)} %bitcast.37), kind=kOutput, calls=%fused_computation.15 | convolution fusion | flops 3246391296 | bytes 7110656 | tf_op jit(solution)/shard_map/me,kec->kmc/dot_general | solution.py:33
  41.0 0.0 copy-done
  41.0 0.0 copy-done.1
  41.0 1.5 fusion.21
  42.5 0.0 all-gather.2.cloned.1.call-update
  42.6 0.0 reduce-scatter.2.cloned.1.call-start
  42.6 122.1 %all-gather.2.cloned.1.call-done = bf16[4096,2048]{1,0:T(8,128)(2,1)} async-done(((bf16[4096,128]{1,0:T(8,128)(2,1)}), bf16[4096,2048]{1,0:T(8,128)(2,1)}) %all-gather.2.cloned.1.call-update) | async-done | bytes 16777232 | tf_op jit(solution)/shard_map/all_gather | solution.py:38
  164.7 11.6 %fusion.24 = f32[2048,128]{1,0:T(8,128)} fusion(bf16[4096,2048]{1,0:T(8,128)(2,1)} %all-gather.2.cloned.1.call-done, bf16[4096,128]{1,0:T(8,128)(2,1)} %fusion.21), kind=kOutput, calls=%fused_computation.28 | convolution fusion | flops 2147483648 | bytes 18874368 | tf_op jit(solution)/shard_map/dot_general | solution.py:15
  176.3 0.0 reduce-scatter.2.cloned.1.call-update
  176.3 37.9 %reduce-scatter.2.cloned.1.call-done = f32[256,128]{1,0:T(8,128)} async-done(((f32[2048,128]{1,0:T(8,128)}), f32[256,128]{1,0:T(8,128)}) %reduce-scatter.2.cloned.1.call-update) | async-done | bytes 131088 | tf_op jit(solution)/shard_map/reduce_scatter | solution.py:39
  214.2 1.6 broadcast_multiply_fusion
Async XLA Ops:
  8.5 18.4 %all-to-all-start = ((bf16[8,3,128,128]{3,2,1,0:T(8,128)(2,1)}), bf16[8,3,128,128]{3,2,1,0:T(8,128)(2,1)S(1)}, u32[]{:S(2)}, u32[]{:S(2)}) async-start(bf16[8,3,128,128]{3,2,1,0:T(8,128)(2,1)} %stack.2), calls=%async_computation | async-start | bytes 1572864 | tf_op jit(solution)/shard_map/all_to_all | solution.py:10
  14.9 149.8 %all-gather.2.cloned.1.call-start = ((), (), s32[]{:S(2)}) async-start(), calls=%async_computation.2 | async-start | bytes 17825792 | tf_op jit(solution)/shard_map/all_gather | solution.py:38
  34.0 7.0 %copy-start = (f32[4096]{0:T(1024)S(1)}, f32[4096]{0:T(1024)}, u32[]{:S(2)}) copy-start(f32[4096]{0:T(1024)} %param.7) | copy-start | bytes 49156
  34.0 7.0 %copy-start.1 = (f32[128]{0:T(128)S(1)}, f32[128]{0:T(128)}, u32[]{:S(2)}) copy-start(f32[128]{0:T(128)} %param.6) | copy-start | bytes 1540
  42.6 171.6 %reduce-scatter.2.cloned.1.call-start = ((), (), s32[]{:S(2)}) async-start(), calls=%async_computation.3 | async-start | bytes 1179648 | tf_op jit(solution)/shard_map/reduce_scatter | solution.py:39
Sparse Core Ops, SparseCore 0:
  42.7 121.9 all-gather.1
  176.4 37.7 reduce-scatter.1
